TPU v7x, 128 devices: a whole 4x4x4 slice. The times are simulated.
128 devices in a mesh: section: 2 (over x_lo), seq: 8 (over y, core), tp: 8 (over z, x_hi).
Axes of the slice: x: 4 (x_hi: 2, x_lo: 2; x = x_hi * 2 + x_lo), y: 4, z: 4, core: 2. Of those that a mesh axis runs over, the one named last changes fastest.
Arguments:
- hidden_image: bfloat16 [2, 1024, 1536], P(None, 'seq'), may hold values from -6 to 6
- hidden_text: bfloat16 [2, 256, 1536], P(None, 'seq'), may hold values from -6 to 6
- latent: float32 [2, 1024, 64], P(None, 'seq'), may hold values from -6 to 6
- timestep: int32 [2], replicated, may hold values from 14 to 27
- text_length: int32 [2], replicated, may hold values from 64 to 154, as said below
- text_keep: int32 [2, 256], replicated, may hold values 0 or 1
- patch_order: int32 [4], replicated, may hold values from 0 to 3, each once
- stale_image_kv: bfloat16 [2, 2, 1024, 2, 1536], P('section', None, 'seq', None, 'tp'), may hold values from -160 to 160
- stale_text_kv: bfloat16 [2, 2, 256, 2, 1536], P('section', None, 'seq', None, 'tp'), may hold values from -6 to 6
- mod_image: float32 [2, 2, 6, 1536], P('section'), may hold values from -3 to 3
- mod_text: float32 [2, 2, 6, 1536], P('section'), may hold values from -3 to 3
- mod_final: float32 [2, 2, 1536], replicated, may hold values from -3 to 3
- qkv_image: bfloat16 [2, 1536, 3, 1536], P('section', None, None, 'tp'), may hold values from -0.15625 to 0.15625
- out_image: bfloat16 [2, 1536, 1536], P('section', 'tp'), may hold values from -0.15625 to 0.15625
- up_image: bfloat16 [2, 1536, 6144], P('section', None, 'tp'), may hold values from -0.15625 to 0.15625
- down_image: bfloat16 [2, 6144, 1536], P('section', 'tp'), may hold values from -0.078125 to 0.078125
- qkv_text: bfloat16 [2, 1536, 3, 1536], P('section', None, None, 'tp'), may hold values from -0.15625 to 0.15625
- out_text: bfloat16 [2, 1536, 1536], P('section', 'tp'), may hold values from -0.15625 to 0.15625
- up_text: bfloat16 [2, 1536, 6144], P('section', None, 'tp'), may hold values from -0.15625 to 0.15625
- down_text: bfloat16 [2, 6144, 1536], P('section', 'tp'), may hold values from -0.078125 to 0.078125
- final_weight: bfloat16 [1536, 64], replicated, may hold values from -0.3125 to 0.3125
Outputs:
- latent_out: float32 [2, 2, 1024, 64], P('section', None, 'seq')
- image_kv_next: bfloat16 [2, 2, 1024, 2, 1536], P('section', None, 'seq', None, 'tp')
- text_kv_next: bfloat16 [2, 2, 256, 2, 1536], P('section', None, 'seq', None, 'tp')
- text_hidden: bfloat16 [2, 2, 256, 1536], P('section', None, 'seq')
Inputs may be any that keep to these rules, and one draw needn't show every extreme that they name: `text_length`: some request has exactly 154 text tokens.
All inputs are finite; a program needn't handle non-finite values.
Results may differ from a plain program's by a relative error of at most 0.023.
Values may be sent and summed in bfloat16 or wider, within the bound.
No kernel may reach another device: no remote copies, remote signals or barrier semaphores. Data moves between devices by JAX's collectives and lax.ppermute only.
A program may use at most 128 MiB of HBM per device.

v0:
```python
import jax
import jax.numpy as jnp
from jax import lax
from jax.sharding import PartitionSpec as P

HD = 64
STEPS = 28
EPSILON = 1e-06
NEGATIVE = -1e30
TIME_SHIFT = 3.0


def passed_along(value, axis, steps):
    count = lax.axis_size(axis)
    initial, last = (max(0, -steps), min(count, count - steps))
    return lax.ppermute(value, axis, [(source, source + steps) for source in range(initial, last)])


def row_norm(values, shift_rows, scale_rows):
    mean_value = jnp.mean(values, axis=-1, keepdims=True)
    centred = values - mean_value
    variance = jnp.mean(centred * centred, axis=-1, keepdims=True)
    return centred * lax.rsqrt(variance + EPSILON) * (1.0 + scale_rows) + shift_rows


def expand_rows(vectors, row_count):
    return jnp.broadcast_to(
        vectors[:, None, :], (vectors.shape[0], row_count, vectors.shape[1])
    ).reshape(-1, vectors.shape[1])


def project(rows, shift_rows, scale_rows, weight):
    flattened = rows.reshape(-1, rows.shape[-1]).astype(jnp.float32)
    normed = row_norm(flattened, shift_rows, scale_rows).astype(jnp.bfloat16)
    mixed = jnp.dot(
        normed, weight.reshape(weight.shape[0], -1), preferred_element_type=jnp.float32
    ).astype(jnp.bfloat16)
    return mixed.reshape(rows.shape[0], rows.shape[1], 3, -1)


def split_heads(values):
    return values.reshape(values.shape[0], values.shape[1], -1, HD)


def block_scores(queries, keys_block, key_mask):
    scores = jnp.einsum(
        "rqhe,rkhe->rhqk", queries, keys_block, preferred_element_type=jnp.float32
    ) * HD ** (-0.5)
    return jnp.where(key_mask[:, None, None, :], scores, NEGATIVE)


def block_weights(scores, rowmax, values_block, key_mask):
    exponent = jnp.where(key_mask[:, None, None, :], jnp.exp(scores - rowmax[..., None]), 0.0)
    totals = jnp.sum(exponent, axis=-1)
    summed = jnp.einsum(
        "rhqk,rkhe->rhqe",
        exponent.astype(jnp.bfloat16),
        values_block,
        preferred_element_type=jnp.float32,
    )
    return (totals, summed)


def heads_out(totals, summed):
    result = summed / totals[..., None]
    merged = jnp.transpose(result, (0, 2, 1, 3))
    return merged.reshape(result.shape[0], result.shape[2], -1).astype(jnp.bfloat16)


def sigma_of(index_value):
    progress = 1.0 - index_value / STEPS
    return TIME_SHIFT * progress / (1.0 + (TIME_SHIFT - 1.0) * progress)


def on_device(
    hidden_image,
    hidden_text,
    latent,
    timestep,
    text_length,
    text_keep,
    patch_order,
    stale_image_kv,
    stale_text_kv,
    mod_image,
    mod_text,
    mod_final,
    qkv_image,
    out_image,
    up_image,
    down_image,
    qkv_text,
    out_text,
    up_text,
    down_text,
    final_weight,
):
    requests = hidden_image.shape[0]
    model_width = hidden_image.shape[2]
    slot_count = patch_order.shape[0]
    image_local = hidden_image.shape[1]
    text_local = hidden_text.shape[1]
    patch_rows = image_local // slot_count
    group_rows = text_local // slot_count
    slot_rows = patch_rows + group_rows
    local_width = qkv_image.shape[3]
    seq_count = lax.axis_size("seq")
    section_index = lax.axis_index("section")
    first_section = section_index == 0
    text_total = text_keep.shape[1]
    positions = jnp.arange(text_total, dtype=jnp.int32)
    valid_text = (positions[None, :] < text_length[:, None]) & (text_keep == 1)
    stale_image, stale_text = (
        lax.all_gather(stale_image_kv[0], "seq", axis=1, tiled=True),
        lax.all_gather(stale_text_kv[0], "seq", axis=1, tiled=True),
    )
    image_buffer = stale_image.reshape(requests, seq_count, slot_count, patch_rows, 2, local_width)
    text_buffer = stale_text.reshape(requests, seq_count, slot_count, group_rows, 2, local_width)
    image_mrows = [expand_rows(mod_image[0][:, column], patch_rows) for column in range(6)]
    text_mrows = [expand_rows(mod_text[0][:, column], group_rows) for column in range(6)]
    image_input = hidden_image.reshape(requests, slot_count, patch_rows, model_width)
    text_input = hidden_text.reshape(requests, slot_count, group_rows, model_width)
    image_store = jnp.zeros((requests, slot_count, patch_rows, model_width), jnp.bfloat16)
    text_store = jnp.zeros((requests, slot_count, group_rows, model_width), jnp.bfloat16)
    image_kv_store = jnp.zeros((requests, slot_count, patch_rows, 2, local_width), jnp.bfloat16)
    text_kv_store = jnp.zeros((requests, slot_count, group_rows, 2, local_width), jnp.bfloat16)
    arrived_image = jnp.zeros((requests, patch_rows, model_width), jnp.bfloat16)
    arrived_text = jnp.zeros((requests, group_rows, model_width), jnp.bfloat16)
    for moment in range(slot_count + 1):
        slot_raw = moment - section_index
        in_range = (slot_raw >= 0) & (slot_raw < slot_count)
        slot_index = jnp.clip(slot_raw, 0, slot_count - 1)
        patch_index = lax.dynamic_index_in_dim(patch_order, slot_index, 0, keepdims=False)
        image_rows = jnp.where(
            first_section,
            lax.dynamic_index_in_dim(image_input, patch_index, 1, keepdims=False),
            arrived_image,
        )
        text_rows = jnp.where(
            first_section,
            lax.dynamic_index_in_dim(text_input, slot_index, 1, keepdims=False),
            arrived_text,
        )
        image_qkv = project(image_rows, image_mrows[0], image_mrows[1], qkv_image[0])
        text_qkv = project(text_rows, text_mrows[0], text_mrows[1], qkv_text[0])
        fresh_local = jnp.concatenate([image_qkv[:, :, 1:], text_qkv[:, :, 1:]], axis=1)
        queries = split_heads(jnp.concatenate([image_qkv[:, :, 0], text_qkv[:, :, 0]], axis=1))
        fresh_all = lax.all_gather(fresh_local, "seq", axis=1, tiled=True)
        fresh_split = fresh_all.reshape(requests, seq_count, slot_rows, 2, local_width)
        image_buffer = lax.dynamic_update_slice_in_dim(
            image_buffer, fresh_split[:, :, None, :patch_rows], patch_index, axis=2
        )
        text_buffer = lax.dynamic_update_slice_in_dim(
            text_buffer, fresh_split[:, :, None, patch_rows:], slot_index, axis=2
        )
        image_keys = image_buffer.reshape(requests, -1, 2, local_width)
        text_keys = text_buffer.reshape(requests, -1, 2, local_width)
        image_mask = jnp.ones((requests, image_keys.shape[1]), jnp.bool_)
        image_scores = block_scores(queries, split_heads(image_keys[:, :, 0]), image_mask)
        text_scores = block_scores(queries, split_heads(text_keys[:, :, 0]), valid_text)
        rowmax = jnp.maximum(jnp.max(image_scores, axis=-1), jnp.max(text_scores, axis=-1))
        image_totals, image_summed = block_weights(
            image_scores, rowmax, split_heads(image_keys[:, :, 1]), image_mask
        )
        text_totals, text_summed = block_weights(
            text_scores, rowmax, split_heads(text_keys[:, :, 1]), valid_text
        )
        attended = heads_out(image_totals + text_totals, image_summed + text_summed)
        image_part = jnp.dot(
            attended[:, :patch_rows].reshape(-1, local_width),
            out_image[0],
            preferred_element_type=jnp.float32,
        )
        text_part = jnp.dot(
            attended[:, patch_rows:].reshape(-1, local_width),
            out_text[0],
            preferred_element_type=jnp.float32,
        )
        image_flat = image_rows.reshape(-1, model_width).astype(jnp.float32)
        text_flat = text_rows.reshape(-1, model_width).astype(jnp.float32)
        image_sum, text_sum = (
            lax.psum(image_part.astype(jnp.bfloat16), "tp").astype(jnp.float32),
            lax.psum(text_part.astype(jnp.bfloat16), "tp").astype(jnp.float32),
        )
        image_first = image_flat + image_mrows[2] * image_sum
        text_first = text_flat + text_mrows[2] * text_sum
        image_normed = row_norm(image_first, image_mrows[3], image_mrows[4]).astype(jnp.bfloat16)
        text_normed = row_norm(text_first, text_mrows[3], text_mrows[4]).astype(jnp.bfloat16)
        image_hidden = jax.nn.gelu(
            jnp.dot(image_normed, up_image[0], preferred_element_type=jnp.float32), approximate=True
        ).astype(jnp.bfloat16)
        text_hidden_rows = jax.nn.gelu(
            jnp.dot(text_normed, up_text[0], preferred_element_type=jnp.float32), approximate=True
        ).astype(jnp.bfloat16)
        image_down, text_down = (
            lax.psum(
                jnp.dot(image_hidden, down_image[0], preferred_element_type=jnp.float32).astype(
                    jnp.bfloat16
                ),
                "tp",
            ).astype(jnp.float32),
            lax.psum(
                jnp.dot(text_hidden_rows, down_text[0], preferred_element_type=jnp.float32).astype(
                    jnp.bfloat16
                ),
                "tp",
            ).astype(jnp.float32),
        )
        image_new = (image_first + image_mrows[5] * image_down).astype(jnp.bfloat16)
        text_new = (text_first + text_mrows[5] * text_down).astype(jnp.bfloat16)
        image_new_rows = image_new.reshape(requests, patch_rows, model_width)
        text_new_rows = text_new.reshape(requests, group_rows, model_width)
        image_store = jnp.where(
            in_range,
            lax.dynamic_update_index_in_dim(image_store, image_new_rows, patch_index, 1),
            image_store,
        )
        text_store = jnp.where(
            in_range,
            lax.dynamic_update_index_in_dim(text_store, text_new_rows, slot_index, 1),
            text_store,
        )
        image_kv_store = jnp.where(
            in_range,
            lax.dynamic_update_index_in_dim(image_kv_store, image_qkv[:, :, 1:], patch_index, 1),
            image_kv_store,
        )
        text_kv_store = jnp.where(
            in_range,
            lax.dynamic_update_index_in_dim(text_kv_store, text_qkv[:, :, 1:], slot_index, 1),
            text_kv_store,
        )
        if moment < slot_count:
            arrived_image, arrived_text = passed_along(
                (image_new_rows, text_new_rows), "section", 1
            )
    final_rows = image_store.reshape(-1, model_width).astype(jnp.float32)
    final_normed = row_norm(
        final_rows,
        expand_rows(mod_final[:, 0], image_local),
        expand_rows(mod_final[:, 1], image_local),
    ).astype(jnp.bfloat16)
    velocity = jnp.dot(final_normed, final_weight, preferred_element_type=jnp.float32).reshape(
        requests, image_local, -1
    )
    returned = passed_along(velocity.astype(jnp.bfloat16), "section", -1).astype(velocity.dtype)
    velocity_used = jnp.where(first_section, returned, velocity)
    index_value = timestep.astype(jnp.float32)
    sigma_now = sigma_of(index_value)
    sigma_next = sigma_of(index_value + 1.0)
    stepped = latent + (sigma_next - sigma_now)[:, None, None] * velocity_used
    denoised = latent - sigma_now[:, None, None] * velocity_used
    latent_part = jnp.where(first_section, stepped, denoised)[None]
    return (
        latent_part,
        image_kv_store.reshape(requests, image_local, 2, local_width)[None],
        text_kv_store.reshape(requests, text_local, 2, local_width)[None],
        text_store.reshape(requests, text_local, model_width)[None],
    )


def solution(mesh):
    in_specs = (
        P(None, "seq", None),
        P(None, "seq", None),
        P(None, "seq", None),
        P(),
        P(),
        P(),
        P(),
        P("section", None, "seq", None, "tp"),
        P("section", None, "seq", None, "tp"),
        P("section", None, None, None),
        P("section", None, None, None),
        P(),
        P("section", None, None, "tp"),
        P("section", "tp", None),
        P("section", None, "tp"),
        P("section", "tp", None),
        P("section", None, None, "tp"),
        P("section", "tp", None),
        P("section", None, "tp"),
        P("section", "tp", None),
        P(),
    )
    out_specs = (
        P("section", None, "seq", None),
        P("section", None, "seq", None, "tp"),
        P("section", None, "seq", None, "tp"),
        P("section", None, "seq", None),
    )
    return jax.shard_map(
        on_device, mesh=mesh, in_specs=in_specs, out_specs=out_specs, check_vma=False
    )
```

profile of v0, /device:TPU:2, one launch (start us, length us, event | category | flops | bytes accessed | tf_op | source)
XLA Modules:
  0.0 1606.8 jit_solution(7978806751904991760)
XLA Ops:
  25.3 14.3 all-gather.1
  94.2 42.6 %psum.142 = bf16[16,1536]{1,0:T(8,128)(2,1)S(1)} all-reduce(bf16[16,1536]{1,0:T(8,128)(2,1)S(1)} %convolution_convert_fusion.9), channel_id=1, replica_groups=mesh['section'=2,'seq'=8,'tp'=8] {'tp'}, use_global_device_ids=true, to_apply=%region_14.15 | all-reduce | flops 24576 | bytes 98304 | tf_op jit(solution)/shard_map/psum | solution.py:183
  140.6 38.1 %psum.143 = bf16[16,1536]{1,0:T(8,128)(2,1)} all-reduce(bf16[16,1536]{1,0:T(8,128)(2,1)S(1)} %fusion.55), channel_id=1, replica_groups=mesh['section'=2,'seq'=8,'tp'=8] {'tp'}, use_global_device_ids=true, to_apply=%region_17.18 | all-reduce | flops 24576 | bytes 98304 | tf_op jit(solution)/shard_map/psum | solution.py:202
  191.2 77.5 %all-reduce.11.cloned.1.call-done = bf16[64,1536]{1,0:T(8,128)(2,1)} async-done(((bf16[64,1536]{1,0:T(8,128)(2,1)}), bf16[64,1536]{1,0:T(8,128)(2,1)}) %all-reduce.11.cloned.1.call-update) | async-done | bytes 196624 | tf_op jit(solution)/shard_map/psum | solution.py:182
  276.6 81.9 %all-reduce.13.cloned.1.call-done = bf16[64,1536]{1,0:T(8,128)(2,1)} async-done(((bf16[64,1536]{1,0:T(8,128)(2,1)}), bf16[64,1536]{1,0:T(8,128)(2,1)}) %all-reduce.13.cloned.1.call-update) | async-done | bytes 196624 | tf_op jit(solution)/shard_map/psum | solution.py:196
  372.8 13.6 all_gather.24
  414.5 39.5 %psum.146 = bf16[16,1536]{1,0:T(8,128)(2,1)S(1)} all-reduce(bf16[16,1536]{1,0:T(8,128)(2,1)S(1)} %convolution_convert_fusion.8), channel_id=1, replica_groups=mesh['section'=2,'seq'=8,'tp'=8] {'tp'}, use_global_device_ids=true, to_apply=%region_30.31 | all-reduce | flops 24576 | bytes 98304 | tf_op jit(solution)/shard_map/psum | solution.py:183
  458.4 40.0 %psum.147 = bf16[16,1536]{1,0:T(8,128)(2,1)} all-reduce(bf16[16,1536]{1,0:T(8,128)(2,1)} %fusion.58), channel_id=1, replica_groups=mesh['section'=2,'seq'=8,'tp'=8] {'tp'}, use_global_device_ids=true, to_apply=%region_33.34 | all-reduce | flops 24576 | bytes 98304 | tf_op jit(solution)/shard_map/psum | solution.py:202
  510.7 77.7 %all-reduce.15.cloned.1.call-done = bf16[64,1536]{1,0:T(8,128)(2,1)} async-done(((bf16[64,1536]{1,0:T(8,128)(2,1)}), bf16[64,1536]{1,0:T(8,128)(2,1)}) %all-reduce.15.cloned.1.call-update) | async-done | bytes 196624 | tf_op jit(solution)/shard_map/psum | solution.py:182
  597.5 80.7 %all-reduce.17.cloned.1.call-done = bf16[64,1536]{1,0:T(8,128)(2,1)} async-done(((bf16[64,1536]{1,0:T(8,128)(2,1)}), bf16[64,1536]{1,0:T(8,128)(2,1)}) %all-reduce.17.cloned.1.call-update) | async-done | bytes 196624 | tf_op jit(solution)/shard_map/psum | solution.py:196
  692.5 13.8 all_gather.25
  734.4 39.5 %psum.150 = bf16[16,1536]{1,0:T(8,128)(2,1)S(1)} all-reduce(bf16[16,1536]{1,0:T(8,128)(2,1)S(1)} %convolution_convert_fusion.7), channel_id=1, replica_groups=mesh['section'=2,'seq'=8,'tp'=8] {'tp'}, use_global_device_ids=true, to_apply=%region_46.47 | all-reduce | flops 24576 | bytes 98304 | tf_op jit(solution)/shard_map/psum | solution.py:183
  778.3 40.0 %psum.151 = bf16[16,1536]{1,0:T(8,128)(2,1)} all-reduce(bf16[16,1536]{1,0:T(8,128)(2,1)} %fusion.61), channel_id=1, replica_groups=mesh['section'=2,'seq'=8,'tp'=8] {'tp'}, use_global_device_ids=true, to_apply=%region_49.50 | all-reduce | flops 24576 | bytes 98304 | tf_op jit(solution)/shard_map/psum | solution.py:202
  830.6 77.7 %all-reduce.19.cloned.1.call-done = bf16[64,1536]{1,0:T(8,128)(2,1)} async-done(((bf16[64,1536]{1,0:T(8,128)(2,1)}), bf16[64,1536]{1,0:T(8,128)(2,1)}) %all-reduce.19.cloned.1.call-update) | async-done | bytes 196624 | tf_op jit(solution)/shard_map/psum | solution.py:182
  917.3 80.7 %all-reduce.21.cloned.1.call-done = bf16[64,1536]{1,0:T(8,128)(2,1)} async-done(((bf16[64,1536]{1,0:T(8,128)(2,1)}), bf16[64,1536]{1,0:T(8,128)(2,1)}) %all-reduce.21.cloned.1.call-update) | async-done | bytes 196624 | tf_op jit(solution)/shard_map/psum | solution.py:196
  1054.0 39.7 %psum.154 = bf16[16,1536]{1,0:T(8,128)(2,1)S(1)} all-reduce(bf16[16,1536]{1,0:T(8,128)(2,1)S(1)} %convolution_convert_fusion.6), channel_id=1, replica_groups=mesh['section'=2,'seq'=8,'tp'=8] {'tp'}, use_global_device_ids=true, to_apply=%region_62.63 | all-reduce | flops 24576 | bytes 98304 | tf_op jit(solution)/shard_map/psum | solution.py:183
  1098.2 40.0 %psum.155 = bf16[16,1536]{1,0:T(8,128)(2,1)} all-reduce(bf16[16,1536]{1,0:T(8,128)(2,1)} %fusion.64), channel_id=1, replica_groups=mesh['section'=2,'seq'=8,'tp'=8] {'tp'}, use_global_device_ids=true, to_apply=%region_65.66 | all-reduce | flops 24576 | bytes 98304 | tf_op jit(solution)/shard_map/psum | solution.py:202
  1149.1 79.0 %all-reduce.23.cloned.1.call-done = bf16[64,1536]{1,0:T(8,128)(2,1)} async-done(((bf16[64,1536]{1,0:T(8,128)(2,1)}), bf16[64,1536]{1,0:T(8,128)(2,1)}) %all-reduce.23.cloned.1.call-update) | async-done | bytes 196624 | tf_op jit(solution)/shard_map/psum | solution.py:182
  1238.0 79.9 %all-reduce.25.cloned.1.call-done = bf16[64,1536]{1,0:T(8,128)(2,1)} async-done(((bf16[64,1536]{1,0:T(8,128)(2,1)}), bf16[64,1536]{1,0:T(8,128)(2,1)}) %all-reduce.25.cloned.1.call-update) | async-done | bytes 196624 | tf_op jit(solution)/shard_map/psum | solution.py:196
  1332.2 13.6 all_gather.27
  1374.0 39.5 %psum.158 = bf16[16,1536]{1,0:T(8,128)(2,1)S(1)} all-reduce(bf16[16,1536]{1,0:T(8,128)(2,1)S(1)} %convolution_convert_fusion.5), channel_id=1, replica_groups=mesh['section'=2,'seq'=8,'tp'=8] {'tp'}, use_global_device_ids=true, to_apply=%region_78.79 | all-reduce | flops 24576 | bytes 98304 | tf_op jit(solution)/shard_map/psum | solution.py:183
  1419.9 39.8 %psum.159 = bf16[16,1536]{1,0:T(8,128)(2,1)} all-reduce(bf16[16,1536]{1,0:T(8,128)(2,1)} %fusion.67), channel_id=1, replica_groups=mesh['section'=2,'seq'=8,'tp'=8] {'tp'}, use_global_device_ids=true, to_apply=%region_81.82 | all-reduce | flops 24576 | bytes 98304 | tf_op jit(solution)/shard_map/psum | solution.py:202
  1459.7 36.9 %all-reduce.27.cloned.1.call-done = bf16[64,1536]{1,0:T(8,128)(2,1)} async-done(((bf16[64,1536]{1,0:T(8,128)(2,1)}), bf16[64,1536]{1,0:T(8,128)(2,1)}) %all-reduce.27.cloned.1.call-update) | async-done | bytes 196624 | tf_op jit(solution)/shard_map/psum | solution.py:182
  1505.8 80.6 %all-reduce.29.cloned.1.call-done = bf16[64,1536]{1,0:T(8,128)(2,1)} async-done(((bf16[64,1536]{1,0:T(8,128)(2,1)}), bf16[64,1536]{1,0:T(8,128)(2,1)}) %all-reduce.29.cloned.1.call-update) | async-done | bytes 196624 | tf_op jit(solution)/shard_map/psum | solution.py:196
  (591 shorter events, 374.8 us)
Async XLA Ops:
  7.2 265.6 %copy-start = (bf16[1,768,1536]{2,1,0:T(8,128)(2,1)S(1)}, bf16[1,768,1536]{2,1,0:T(8,128)(2,1)}, u32[]{:S(2)}) copy-start(bf16[1,768,1536]{2,1,0:T(8,128)(2,1)} %param.36) | copy-start | bytes 7077892
  7.2 73.1 %all-gather.4.cloned.1.call-start = ((), (), s32[]{:S(2)}) async-start(), calls=%async_computation.10 | async-start | bytes 2359296 | tf_op jit(solution)/shard_map/all_gather | solution.py:114
  9.2 259.5 %all-reduce.11.cloned.1.call-start = ((), (), s32[]{:S(2)}) async-start(), calls=%async_computation | async-start | bytes 393216 | tf_op jit(solution)/shard_map/psum | solution.py:182
  180.3 6.3 collective-permute-start.1
  183.3 175.3 %all-reduce.13.cloned.1.call-start = ((), (), s32[]{:S(2)}) async-start(), calls=%async_computation.1 | async-start | bytes 393216 | tf_op jit(solution)/shard_map/psum | solution.py:196
  276.5 312.0 %all-reduce.15.cloned.1.call-start = ((), (), s32[]{:S(2)}) async-start(), calls=%async_computation.2 | async-start | bytes 393216 | tf_op jit(solution)/shard_map/psum | solution.py:182
  359.7 7.6 collective-permute-start
  458.4 132.2 %copy-start.74 = (f32[2,1536]{1,0:T(2,128)S(1)}, f32[2,1536]{1,0:T(2,128)}, u32[]{:S(2)}) copy-start(f32[2,1536]{1,0:T(2,128)} %get-tuple-element.117) | copy-start | bytes 36868
  458.4 132.3 %copy-start.79 = (f32[2,1536]{1,0:T(2,128)S(1)}, f32[2,1536]{1,0:T(2,128)}, u32[]{:S(2)}) copy-start(f32[2,1536]{1,0:T(2,128)} %get-tuple-element.118) | copy-start | bytes 36868
  499.9 6.2 collective-permute-start.3
  504.9 173.3 %all-reduce.17.cloned.1.call-start = ((), (), s32[]{:S(2)}) async-start(), calls=%async_computation.3 | async-start | bytes 393216 | tf_op jit(solution)/shard_map/psum | solution.py:196
  596.1 312.2 %all-reduce.19.cloned.1.call-start = ((), (), s32[]{:S(2)}) async-start(), calls=%async_computation.4 | async-start | bytes 393216 | tf_op jit(solution)/shard_map/psum | solution.py:182
  679.4 7.6 collective-permute-start.2
  778.3 132.2 %copy-start.80 = (f32[2,1536]{1,0:T(2,128)S(1)}, f32[2,1536]{1,0:T(2,128)}, u32[]{:S(2)}) copy-start(f32[2,1536]{1,0:T(2,128)} %get-tuple-element.118) | copy-start | bytes 36868
  819.8 6.2 collective-permute-start.5
  824.7 173.2 %all-reduce.21.cloned.1.call-start = ((), (), s32[]{:S(2)}) async-start(), calls=%async_computation.5 | async-start | bytes 393216 | tf_op jit(solution)/shard_map/psum | solution.py:196
  915.9 312.2 %all-reduce.23.cloned.1.call-start = ((), (), s32[]{:S(2)}) async-start(), calls=%async_computation.6 | async-start | bytes 393216 | tf_op jit(solution)/shard_map/psum | solution.py:182
  999.2 7.6 collective-permute-start.4
  1139.6 6.2 collective-permute-start.7
  1144.6 173.3 %all-reduce.25.cloned.1.call-start = ((), (), s32[]{:S(2)}) async-start(), calls=%async_computation.7 | async-start | bytes 393216 | tf_op jit(solution)/shard_map/psum | solution.py:196
  1235.8 260.9 %all-reduce.27.cloned.1.call-start = ((), (), s32[]{:S(2)}) async-start(), calls=%async_computation.8 | async-start | bytes 393216 | tf_op jit(solution)/shard_map/psum | solution.py:182
  1319.1 7.6 collective-permute-start.6
  1415.8 170.6 %all-reduce.29.cloned.1.call-start = ((), (), s32[]{:S(2)}) async-start(), calls=%async_computation.9 | async-start | bytes 393216 | tf_op jit(solution)/shard_map/psum | solution.py:196
  1591.9 7.4 collective-permute-start.8
  (101 other events, 4056.7 us)
Sparse Core Ops, SparseCore 0:
  9.7 28.3 all-gather.3
  183.4 85.3 all-reduce.10
  276.6 81.8 all-reduce.12
  505.0 83.3 all-reduce.14
  596.2 81.8 all-reduce.16
  824.9 83.3 all-reduce.18
  916.0 81.8 all-reduce.20
  1144.7 83.3 all-reduce.22
  1235.9 81.8 all-reduce.24
  1415.9 80.6 all-reduce.26
  1504.5 81.8 all-reduce.28
where the time goes:
time: 1620 us; the launch traced here: 1610 us
  waiting for transfers between devices  784 us (48%)
  blocking collectives  481 us (30%)
  local copies, waits for them, and re-layouts  130 us (8%)
  matrix products  100 us (6%)
  other arithmetic  72.3 us (4%)
  between operations  25.4 us (2%)
    psum x5, waiting for transfers between devices, on_device(): lax.psum(jnp.dot(image_hidden, down_image[0], preferred_element_type=jnp....  404 us
    psum x5, waiting for transfers between devices, on_device(): lax.psum(image_part.astype(jnp.bfloat16), 'tp').astype(jnp.float32)  349 us
    psum x5, blocking collectives, on_device(): lax.psum(text_part.astype(jnp.bfloat16), 'tp').astype(jnp.float32)  201 us
    psum x5, blocking collectives, on_device(): lax.psum(jnp.dot(text_hidden_rows, down_text[0], preferred_element_type=j...  198 us
    all_gather x5, blocking collectives, on_device(): fresh_all = lax.all_gather(fresh_local, 'seq', axis=1, tiled=True)  67.8 us
  transfers between devices with their start and end apart: 20, of which 18 were waited for; matrix products, arithmetic and copies ran while one was open for 5% of the time, Pallas kernels for 0%

commit v1 on v0

--- a/solution.py
+++ b/solution.py
@@ -145,7 +145,25 @@
         text_qkv = project(text_rows, text_mrows[0], text_mrows[1], qkv_text[0])
         fresh_local = jnp.concatenate([image_qkv[:, :, 1:], text_qkv[:, :, 1:]], axis=1)
         queries = split_heads(jnp.concatenate([image_qkv[:, :, 0], text_qkv[:, :, 0]], axis=1))
-        fresh_all = lax.all_gather(fresh_local, "seq", axis=1, tiled=True)
+        ways, here, step = (lax.axis_size("seq"), lax.axis_index("seq"), fresh_local.shape[1])
+        lengths = [n * ways if d == 1 else n for d, n in enumerate(fresh_local.shape)]
+        full = lax.dynamic_update_slice_in_dim(
+            jnp.zeros(lengths, fresh_local.dtype), fresh_local, here * step, axis=1
+        )
+        going_up = going_down = fresh_local
+        for far in range(1, ways // 2 + 1):
+            going_up = lax.ppermute(going_up, "seq", [(d, (d + 1) % ways) for d in range(ways)])
+            full = lax.dynamic_update_slice_in_dim(
+                full, going_up, (here - far) % ways * step, axis=1
+            )
+            if 2 * far < ways:
+                going_down = lax.ppermute(
+                    going_down, "seq", [(d, (d - 1) % ways) for d in range(ways)]
+                )
+                full = lax.dynamic_update_slice_in_dim(
+                    full, going_down, (here + far) % ways * step, axis=1
+                )
+        fresh_all = full
         fresh_split = fresh_all.reshape(requests, seq_count, slot_rows, 2, local_width)
         image_buffer = lax.dynamic_update_slice_in_dim(
             image_buffer, fresh_split[:, :, None, :patch_rows], patch_index, axis=2

time: 1620 us -> 1670 us (1.031)
  blocking collectives: 481 us -> 413 us
  local copies, waits for them, and re-layouts: 130 us -> 187 us
  starting transfers between devices: 14.6 us -> 59.2 us
    all_gather x5 -> x0, blocking collectives: 67.8 us -> none  [on_device(): fresh_all = lax.all_gather(fresh_local, 'seq', axis=1, tiled=True)]
    psum x5, waiting for transfers between devices: 404 us -> 359 us  [on_device(): lax.psum(jnp.dot(image_hidden, down_image[0], preferred_element_type=jnp....]
    ppermute x0 -> x35, starting transfers between devices: none -> 44.3 us  [the longest x15 43.9 us: on_device(): lax.ppermute(going_down, 'seq', [(d, (d - 1) % ways) for d in range(ways)])]
    dynamic_update_slice x0 -> x40, local copies, waits for them, and re-layouts: none -> 39.3 us  [the longest x20 17.4 us: on_device(): lax.dynamic_update_slice_in_dim(full, going_up, (here - far) % ways * ste...]
    psum x5, waiting for transfers between devices: 349 us -> 375 us  [on_device(): lax.psum(image_part.astype(jnp.bfloat16), 'tp').astype(jnp.float32)]
    ppermute x0 -> x35, waiting for transfers between devices: none -> 23.2 us  [the longest x20 22.3 us: on_device(): lax.ppermute(going_up, 'seq', [(d, (d + 1) % ways) for d in range(ways)])]
  transfers between devices with their start and end apart: 20 -> 55, of which waited for: 18 -> 37; matrix products, arithmetic and copies ran while one was open for 5% -> 8% of each run, Pallas kernels for 0% -> 0%
where the time goes in v1:
time: 1670 us; the launch traced here: 1650 us
  waiting for transfers between devices  794 us (48%)
  blocking collectives  413 us (25%)
  local copies, waits for them, and re-layouts  187 us (11%)
  matrix products  102 us (6%)
  other arithmetic  72.7 us (4%)
  starting transfers between devices  59.2 us (4%)
  between operations  25.3 us (2%)
    psum x5, waiting for transfers between devices, on_device(): lax.psum(image_part.astype(jnp.bfloat16), 'tp').astype(jnp.float32)  375 us
    psum x5, waiting for transfers between devices, on_device(): lax.psum(jnp.dot(image_hidden, down_image[0], preferred_element_type=jnp....  359 us
    psum x5, blocking collectives, on_device(): lax.psum(text_part.astype(jnp.bfloat16), 'tp').astype(jnp.float32)  201 us
    psum x5, blocking collectives, on_device(): lax.psum(jnp.dot(text_hidden_rows, down_text[0], preferred_element_type=j...  198 us
    ppermute x15, starting transfers between devices, on_device(): lax.ppermute(going_down, 'seq', [(d, (d - 1) % ways) for d in range(ways)])  43.9 us
    ppermute x9, waiting for transfers between devices, passed_along(): lax.ppermute(value, axis, [(source, source + steps) for source in range(i...  36.8 us
  transfers between devices with their start and end apart: 55, of which 37 were waited for; matrix products, arithmetic and copies ran while one was open for 8% of the time, Pallas kernels for 0%

profile of v1, /device:TPU:2, one launch (start us, length us, event | category | flops | bytes accessed | tf_op | source)
XLA Modules:
  0.0 1653.7 jit_solution(13675003534327708894)
XLA Ops:
  34.2 13.9 all-gather.1
  96.0 42.8 %psum.142 = bf16[16,1536]{1,0:T(8,128)(2,1)S(1)} all-reduce(bf16[16,1536]{1,0:T(8,128)(2,1)S(1)} %convolution_convert_fusion.9), channel_id=1, replica_groups=mesh['section'=2,'seq'=8,'tp'=8] {'tp'}, use_global_device_ids=true, to_apply=%region_14.15 | all-reduce | flops 24576 | bytes 98304 | tf_op jit(solution)/shard_map/psum | solution.py:201
  142.7 38.1 %psum.143 = bf16[16,1536]{1,0:T(8,128)(2,1)} all-reduce(bf16[16,1536]{1,0:T(8,128)(2,1)S(1)} %fusion.55), channel_id=1, replica_groups=mesh['section'=2,'seq'=8,'tp'=8] {'tp'}, use_global_device_ids=true, to_apply=%region_17.18 | all-reduce | flops 24576 | bytes 98304 | tf_op jit(solution)/shard_map/psum | solution.py:220
  193.1 75.8 %all-reduce.11.cloned.1.call-done = bf16[64,1536]{1,0:T(8,128)(2,1)} async-done(((bf16[64,1536]{1,0:T(8,128)(2,1)}), bf16[64,1536]{1,0:T(8,128)(2,1)}) %all-reduce.11.cloned.1.call-update) | async-done | bytes 196624 | tf_op jit(solution)/shard_map/psum | solution.py:200
  279.4 79.2 %all-reduce.13.cloned.1.call-done = bf16[64,1536]{1,0:T(8,128)(2,1)} async-done(((bf16[64,1536]{1,0:T(8,128)(2,1)}), bf16[64,1536]{1,0:T(8,128)(2,1)}) %all-reduce.13.cloned.1.call-update) | async-done | bytes 196624 | tf_op jit(solution)/shard_map/psum | solution.py:214
  429.5 39.5 %psum.146 = bf16[16,1536]{1,0:T(8,128)(2,1)S(1)} all-reduce(bf16[16,1536]{1,0:T(8,128)(2,1)S(1)} %convolution_convert_fusion.8), channel_id=1, replica_groups=mesh['section'=2,'seq'=8,'tp'=8] {'tp'}, use_global_device_ids=true, to_apply=%region_30.31 | all-reduce | flops 24576 | bytes 98304 | tf_op jit(solution)/shard_map/psum | solution.py:201
  473.4 39.9 %psum.147 = bf16[16,1536]{1,0:T(8,128)(2,1)} all-reduce(bf16[16,1536]{1,0:T(8,128)(2,1)} %fusion.58), channel_id=1, replica_groups=mesh['section'=2,'seq'=8,'tp'=8] {'tp'}, use_global_device_ids=true, to_apply=%region_33.34 | all-reduce | flops 24576 | bytes 98304 | tf_op jit(solution)/shard_map/psum | solution.py:220
  525.6 74.1 %all-reduce.15.cloned.1.call-done = bf16[64,1536]{1,0:T(8,128)(2,1)} async-done(((bf16[64,1536]{1,0:T(8,128)(2,1)}), bf16[64,1536]{1,0:T(8,128)(2,1)}) %all-reduce.15.cloned.1.call-update) | async-done | bytes 196624 | tf_op jit(solution)/shard_map/psum | solution.py:200
  608.8 80.7 %all-reduce.17.cloned.1.call-done = bf16[64,1536]{1,0:T(8,128)(2,1)} async-done(((bf16[64,1536]{1,0:T(8,128)(2,1)}), bf16[64,1536]{1,0:T(8,128)(2,1)}) %all-reduce.17.cloned.1.call-update) | async-done | bytes 196624 | tf_op jit(solution)/shard_map/psum | solution.py:214
  692.1 6.2 collective-permute-done.16
  760.3 39.7 %psum.150 = bf16[16,1536]{1,0:T(8,128)(2,1)S(1)} all-reduce(bf16[16,1536]{1,0:T(8,128)(2,1)S(1)} %convolution_convert_fusion.7), channel_id=1, replica_groups=mesh['section'=2,'seq'=8,'tp'=8] {'tp'}, use_global_device_ids=true, to_apply=%region_46.47 | all-reduce | flops 24576 | bytes 98304 | tf_op jit(solution)/shard_map/psum | solution.py:201
  804.5 39.9 %psum.151 = bf16[16,1536]{1,0:T(8,128)(2,1)} all-reduce(bf16[16,1536]{1,0:T(8,128)(2,1)} %fusion.61), channel_id=1, replica_groups=mesh['section'=2,'seq'=8,'tp'=8] {'tp'}, use_global_device_ids=true, to_apply=%region_49.50 | all-reduce | flops 24576 | bytes 98304 | tf_op jit(solution)/shard_map/psum | solution.py:220
  856.7 74.1 %all-reduce.19.cloned.1.call-done = bf16[64,1536]{1,0:T(8,128)(2,1)} async-done(((bf16[64,1536]{1,0:T(8,128)(2,1)}), bf16[64,1536]{1,0:T(8,128)(2,1)}) %all-reduce.19.cloned.1.call-update) | async-done | bytes 196624 | tf_op jit(solution)/shard_map/psum | solution.py:200
  939.9 80.7 %all-reduce.21.cloned.1.call-done = bf16[64,1536]{1,0:T(8,128)(2,1)} async-done(((bf16[64,1536]{1,0:T(8,128)(2,1)}), bf16[64,1536]{1,0:T(8,128)(2,1)}) %all-reduce.21.cloned.1.call-update) | async-done | bytes 196624 | tf_op jit(solution)/shard_map/psum | solution.py:214
  1023.2 6.2 collective-permute-done.25
  1091.4 39.5 %psum.154 = bf16[16,1536]{1,0:T(8,128)(2,1)S(1)} all-reduce(bf16[16,1536]{1,0:T(8,128)(2,1)S(1)} %convolution_convert_fusion.6), channel_id=1, replica_groups=mesh['section'=2,'seq'=8,'tp'=8] {'tp'}, use_global_device_ids=true, to_apply=%region_62.63 | all-reduce | flops 24576 | bytes 98304 | tf_op jit(solution)/shard_map/psum | solution.py:201
  1135.3 39.9 %psum.155 = bf16[16,1536]{1,0:T(8,128)(2,1)} all-reduce(bf16[16,1536]{1,0:T(8,128)(2,1)} %fusion.64), channel_id=1, replica_groups=mesh['section'=2,'seq'=8,'tp'=8] {'tp'}, use_global_device_ids=true, to_apply=%region_65.66 | all-reduce | flops 24576 | bytes 98304 | tf_op jit(solution)/shard_map/psum | solution.py:220
  1189.2 73.2 %all-reduce.23.cloned.1.call-done = bf16[64,1536]{1,0:T(8,128)(2,1)} async-done(((bf16[64,1536]{1,0:T(8,128)(2,1)}), bf16[64,1536]{1,0:T(8,128)(2,1)}) %all-reduce.23.cloned.1.call-update) | async-done | bytes 196624 | tf_op jit(solution)/shard_map/psum | solution.py:200
  1272.4 79.8 %all-reduce.25.cloned.1.call-done = bf16[64,1536]{1,0:T(8,128)(2,1)} async-done(((bf16[64,1536]{1,0:T(8,128)(2,1)}), bf16[64,1536]{1,0:T(8,128)(2,1)}) %all-reduce.25.cloned.1.call-update) | async-done | bytes 196624 | tf_op jit(solution)/shard_map/psum | solution.py:214
  1355.0 6.0 collective-permute-done.34
  1426.5 39.5 %psum.158 = bf16[16,1536]{1,0:T(8,128)(2,1)S(1)} all-reduce(bf16[16,1536]{1,0:T(8,128)(2,1)S(1)} %convolution_convert_fusion.5), channel_id=1, replica_groups=mesh['section'=2,'seq'=8,'tp'=8] {'tp'}, use_global_device_ids=true, to_apply=%region_78.79 | all-reduce | flops 24576 | bytes 98304 | tf_op jit(solution)/shard_map/psum | solution.py:201
  1468.9 78.1 %all-reduce.27.cloned.1.call-done = bf16[64,1536]{1,0:T(8,128)(2,1)} async-done(((bf16[64,1536]{1,0:T(8,128)(2,1)}), bf16[64,1536]{1,0:T(8,128)(2,1)}) %all-reduce.27.cloned.1.call-update) | async-done | bytes 196624 | tf_op jit(solution)/shard_map/psum | solution.py:200
  1558.1 40.4 %psum.159 = bf16[16,1536]{1,0:T(8,128)(2,1)} all-reduce(bf16[16,1536]{1,0:T(8,128)(2,1)S(1)} %fusion.67), channel_id=1, replica_groups=mesh['section'=2,'seq'=8,'tp'=8] {'tp'}, use_global_device_ids=true, to_apply=%region_81.82 | all-reduce | flops 24576 | bytes 98304 | tf_op jit(solution)/shard_map/psum | solution.py:220
  1598.5 38.4 %all-reduce.29.cloned.1.call-done = bf16[64,1536]{1,0:T(8,128)(2,1)} async-done(((bf16[64,1536]{1,0:T(8,128)(2,1)}), bf16[64,1536]{1,0:T(8,128)(2,1)}) %all-reduce.29.cloned.1.call-update) | async-done | bytes 196624 | tf_op jit(solution)/shard_map/psum | solution.py:214
  (673 shorter events, 462.6 us)
Async XLA Ops:
  7.2 74.0 %all-gather.4.cloned.1.call-start = ((), (), s32[]{:S(2)}) async-start(), calls=%async_computation.10 | async-start | bytes 2359296 | tf_op jit(solution)/shard_map/all_gather | solution.py:114
  23.3 36.5 %collective-permute-start = (bf16[2,40,2,192]{3,2,1,0:T(2,128)(2,1)}, bf16[2,40,2,192]{3,2,1,0:T(2,128)(2,1)}, u32[]{:S(2)}, u32[]{:S(2)}) collective-permute-start(bf16[2,40,2,192]{3,2,1,0:T(2,128)(2,1)} %pad_maximum_fusion), channel_id=1, source_target_pairs={{0,8},{8,16},{16,24},{24,32},{32,40},{40,48},{48,56},{56,0},{1,9},... | collective-permute-start | bytes 184328 | tf_op jit(solution)/shard_map/ppermute | solution.py:155
  23.3 36.9 %collective-permute-start.1 = (bf16[2,40,2,192]{3,2,1,0:T(2,128)(2,1)}, bf16[2,40,2,192]{3,2,1,0:T(2,128)(2,1)}, u32[]{:S(2)}, u32[]{:S(2)}) collective-permute-start(bf16[2,40,2,192]{3,2,1,0:T(2,128)(2,1)} %pad_maximum_fusion), channel_id=1, source_target_pairs={{0,56},{8,0},{16,8},{24,16},{32,24},{40,32},{48,40},{56,48},{1,57}... | collective-permute-start | bytes 184328 | tf_op jit(solution)/shard_map/ppermute | solution.py:160
  27.1 241.8 %all-reduce.11.cloned.1.call-start = ((), (), s32[]{:S(2)}) async-start(), calls=%async_computation | async-start | bytes 393216 | tf_op jit(solution)/shard_map/psum | solution.py:200
  185.3 173.4 %all-reduce.13.cloned.1.call-start = ((), (), s32[]{:S(2)}) async-start(), calls=%async_computation.1 | async-start | bytes 393216 | tf_op jit(solution)/shard_map/psum | solution.py:214
  276.6 323.2 %all-reduce.15.cloned.1.call-start = ((), (), s32[]{:S(2)}) async-start(), calls=%async_computation.2 | async-start | bytes 393216 | tf_op jit(solution)/shard_map/psum | solution.py:200
  359.9 7.6 collective-permute-start.7
  372.8 12.0 collective-permute-start.9
  372.8 13.5 collective-permute-start.10
  518.1 171.4 %all-reduce.17.cloned.1.call-start = ((), (), s32[]{:S(2)}) async-start(), calls=%async_computation.3 | async-start | bytes 393216 | tf_op jit(solution)/shard_map/psum | solution.py:214
  607.4 323.4 %all-reduce.19.cloned.1.call-start = ((), (), s32[]{:S(2)}) async-start(), calls=%async_computation.4 | async-start | bytes 393216 | tf_op jit(solution)/shard_map/psum | solution.py:200
  690.8 7.6 collective-permute-start.16
  703.7 12.0 collective-permute-start.18
  703.7 13.5 collective-permute-start.19
  849.2 171.4 %all-reduce.21.cloned.1.call-start = ((), (), s32[]{:S(2)}) async-start(), calls=%async_computation.5 | async-start | bytes 393216 | tf_op jit(solution)/shard_map/psum | solution.py:214
  938.5 323.9 %all-reduce.23.cloned.1.call-start = ((), (), s32[]{:S(2)}) async-start(), calls=%async_computation.6 | async-start | bytes 393216 | tf_op jit(solution)/shard_map/psum | solution.py:200
  1034.7 12.0 collective-permute-start.27
  1034.7 13.5 collective-permute-start.28
  1180.1 172.0 %all-reduce.25.cloned.1.call-start = ((), (), s32[]{:S(2)}) async-start(), calls=%async_computation.7 | async-start | bytes 393216 | tf_op jit(solution)/shard_map/psum | solution.py:214
  1270.1 277.0 %all-reduce.27.cloned.1.call-start = ((), (), s32[]{:S(2)}) async-start(), calls=%async_computation.8 | async-start | bytes 393216 | tf_op jit(solution)/shard_map/psum | solution.py:200
  1353.4 7.6 collective-permute-start.34
  1366.3 15.4 collective-permute-start.36
  1366.3 17.0 %collective-permute-start.37 = (bf16[2,40,2,192]{3,2,1,0:T(2,128)(2,1)}, bf16[2,40,2,192]{3,2,1,0:T(2,128)(2,1)}, u32[]{:S(2)}, u32[]{:S(2)}) collective-permute-start(bf16[2,40,2,192]{3,2,1,0:T(2,128)(2,1)} %pad_maximum_fusion.4), channel_id=1, source_target_pairs={{0,56},{8,0},{16,8},{24,16},{32,24},{40,32},{48,40},{56,48},{1,57}... | collective-permute-start | bytes 184328 | tf_op jit(solution)/shard_map/ppermute | solution.py:160
  1468.3 168.6 %all-reduce.29.cloned.1.call-start = ((), (), s32[]{:S(2)}) async-start(), calls=%async_computation.9 | async-start | bytes 393216 | tf_op jit(solution)/shard_map/psum | solution.py:214
  (123 other events, 4651.4 us)
Sparse Core Ops, SparseCore 0:
  27.2 27.0 all-gather.3
  185.4 83.4 all-reduce.10
  276.7 81.8 all-reduce.12
  518.2 81.5 all-reduce.14
  607.5 81.8 all-reduce.16
  849.3 81.4 all-reduce.18
  938.6 81.8 all-reduce.20
  1180.2 82.1 all-reduce.22
  1270.2 81.8 all-reduce.24
  1468.5 78.5 all-reduce.26
  1554.8 82.0 all-reduce.28
